TPU v7x, 32 devices: a whole 2x2x4 slice. The times are simulated.
32 devices in a mesh: ctx: 8 (over z, x), fsdp: 4 (over y, core).
Axes of the slice: x: 2, y: 2, z: 4, core: 2. Of those that a mesh axis runs over, the one named last changes fastest.
Arguments:
- block_in: bfloat16 [4, 2048, 1024], P('fsdp', 'ctx'), may hold values from -6 to 6
- out_grad: bfloat16 [4, 2048, 1024], P('fsdp', 'ctx'), may hold values from -6 to 6
- w_query: bfloat16 [1024, 1024], P('fsdp'), may hold values from -0.1875 to 0.1875
- w_key: bfloat16 [1024, 1024], P('fsdp'), may hold values from -0.1875 to 0.1875
- w_value: bfloat16 [1024, 1024], P('fsdp'), may hold values from -0.1875 to 0.1875
- w_out: bfloat16 [1024, 1024], P('fsdp'), may hold values from -0.1875 to 0.1875
- norm_one: float32 [1024], replicated, may hold values from 0.25 to 1.75
- norm_two: float32 [1024], replicated, may hold values from 0.25 to 1.75
- w_gate: bfloat16 [1024, 2816], P('fsdp'), may hold values from -0.1875 to 0.1875
- w_up: bfloat16 [1024, 2816], P('fsdp'), may hold values from -0.1875 to 0.1875
- w_down: bfloat16 [2816, 1024], P('fsdp'), may hold values from -0.109375 to 0.109375
- norm_three: float32 [1024], replicated, may hold values from 0.25 to 1.75
- norm_four: float32 [1024], replicated, may hold values from 0.25 to 1.75
- prompt_len: int32 [4], replicated, may hold values from 512 to 1024, as said below
- cont_len: int32 [4, 2], replicated, may hold values from 257 to 512, as said below
- group_ids: int32 [4], replicated, may hold values from 0 to 3, each once
- cont_ids: int32 [4, 2], replicated, may hold values from 0 to 1, each once within a row
Outputs:
- block_out: bfloat16 [4, 2048, 1024], P('fsdp', 'ctx')
- in_grad: float32 [4, 2048, 1024], P('fsdp', 'ctx')
- grad_query: float32 [1024, 1024], P('fsdp')
- grad_key: float32 [1024, 1024], P('fsdp')
- grad_value: float32 [1024, 1024], P('fsdp')
- grad_out: float32 [1024, 1024], P('fsdp')
- grad_norm_one: float32 [1024], replicated
- grad_norm_two: float32 [1024], replicated
- grad_gate: float32 [1024, 2816], P('fsdp')
- grad_up: float32 [1024, 2816], P('fsdp')
- grad_down: float32 [2816, 1024], P('fsdp')
- grad_norm_three: float32 [1024], replicated
- grad_norm_four: float32 [1024], replicated
Inputs may be any that keep to these rules, and one draw needn't show every extreme that they name: `prompt_len`: in every draw some group's prompt has exactly 1024 tokens. `cont_len`: every group has a continuation of exactly 512 tokens. `group_ids`: A permutation of the groups. `cont_ids`: each row is a permutation of the continuation numbers.
All inputs are finite; a program needn't handle non-finite values.
Results may differ from a plain program's by a relative error of at most 0.023.
Values may be sent and summed in bfloat16 or wider, within the bound.
No kernel may reach another device: no remote copies, remote signals or barrier semaphores. Data moves between devices by JAX's collectives and lax.ppermute only.
A program may use at most 192 MiB of HBM per device.

v0:
```python
import math
import jax
import jax.numpy as jnp
from jax import lax
from jax.sharding import PartitionSpec as P

HEAD = 128
P_DEV = 128
CONT = 512
eps_norm = 1e-06
rope_base = 50000.0
masked_out = -1e30


def rms_norm(values, gain_vec):
    inverse = lax.rsqrt(jnp.mean(values * values, axis=-1, keepdims=True) + eps_norm)
    return (values * inverse * gain_vec, inverse)


def norm_back(values, inverse, gain_vec, upstream):
    weighted = upstream * gain_vec
    inner_mean = jnp.mean(values * weighted, axis=-1, keepdims=True)
    value_grad = inverse * weighted - values * inverse * inverse * inverse * inner_mean
    return (value_grad, jnp.sum(upstream * values * inverse, axis=0))


def rotate(values, position, turn_sign):
    seq_len = values.shape[0]
    half_size = HEAD // 2
    split_heads = values.reshape(seq_len, -1, HEAD)
    frequencies = rope_base ** (-2.0 * jnp.arange(half_size, dtype=jnp.float32) / HEAD)
    angles = position.astype(jnp.float32)[:, None] * frequencies[None, :]
    cosine = jnp.concatenate([jnp.cos(angles), jnp.cos(angles)], axis=-1)[:, None, :]
    sine_part = turn_sign * jnp.concatenate([jnp.sin(angles), jnp.sin(angles)], axis=-1)[:, None, :]
    turned = jnp.concatenate([-split_heads[..., half_size:], split_heads[..., :half_size]], axis=-1)
    return (split_heads * cosine + turned * sine_part).reshape(seq_len, -1)


def token_info(slot_index, prompt, prompt_size, slot_lens):
    in_cont = slot_index >= prompt
    rel_index = jnp.maximum(slot_index - prompt, 0)
    slot_of = jnp.where(in_cont, rel_index // CONT, -1)
    offset = rel_index % CONT
    slot_range = jnp.arange(slot_lens.shape[0], dtype=jnp.int32)
    slot_len = jnp.sum(
        jnp.where(slot_of[:, None] == slot_range[None, :], slot_lens[None, :], 0), axis=1
    )
    token_valid = jnp.where(in_cont, offset < slot_len, slot_index < prompt_size)
    position = jnp.where(in_cont, prompt_size + offset, slot_index)
    return (token_valid, slot_of, position)


def cross_dot(operand, partner):
    return lax.dot_general(
        operand, partner, (((0,), (0,)), ((), ())), preferred_element_type=jnp.float32
    )


def back_dot(operand, partner):
    return lax.dot_general(
        operand, partner, (((1,), (1,)), ((), ())), preferred_element_type=jnp.float32
    )


def keep_same(state):
    return state


def shards(
    block_in,
    out_grad,
    w_query,
    w_key,
    w_value,
    w_out,
    norm_one,
    norm_two,
    w_gate,
    w_up,
    w_down,
    norm_three,
    norm_four,
    prompt_len,
    cont_len,
    group_ids,
    cont_ids,
):
    local_rows = block_in.shape[1]
    model_width = block_in.shape[2]
    ff_width = w_gate.shape[1]
    ctx_size = lax.axis_size("ctx")
    group_rows = local_rows * ctx_size
    prompt = P_DEV * ctx_size
    head_count = model_width // HEAD
    score_scale = 1.0 / math.sqrt(HEAD)
    row_index = lax.axis_index("fsdp")
    groups = group_ids.shape[0]
    slot_count = cont_ids.shape[1]
    group_range = jnp.arange(groups, dtype=jnp.int32)
    own_group = jnp.sum(jnp.where(group_range == row_index, group_ids, 0))
    own_prompt = jnp.sum(jnp.where(group_range == own_group, prompt_len, 0))
    own_lens = jnp.sum(jnp.where((group_range == own_group)[:, None], cont_len, 0), axis=0)
    own_ids = jnp.sum(jnp.where((group_range == row_index)[:, None], cont_ids, 0), axis=0)
    slot_range = jnp.arange(slot_count, dtype=jnp.int32)
    slot_lens = jnp.sum(
        jnp.where(own_ids[:, None] == slot_range[None, :], own_lens[None, :], 0), axis=1
    )
    query_index = lax.axis_index("ctx") * local_rows + jnp.arange(local_rows, dtype=jnp.int32)
    key_index = jnp.arange(group_rows, dtype=jnp.int32)
    query_valid, query_slot, position = token_info(query_index, prompt, own_prompt, slot_lens)
    key_valid, key_slot, unused_pos = token_info(key_index, prompt, own_prompt, slot_lens)
    tokens = block_in[0].astype(jnp.float32)
    full_query, full_key, full_value, full_out = (
        lax.all_gather(w_query, "fsdp", axis=0, tiled=True),
        lax.all_gather(w_key, "fsdp", axis=0, tiled=True),
        lax.all_gather(w_value, "fsdp", axis=0, tiled=True),
        lax.all_gather(w_out, "fsdp", axis=0, tiled=True),
    )
    normed_full, inverse_one = rms_norm(tokens, norm_one)
    normed = normed_full.astype(jnp.bfloat16)
    queries = rotate(
        jnp.dot(normed, full_query, preferred_element_type=jnp.float32), position, 1.0
    ).astype(jnp.bfloat16)
    keys_local = rotate(
        jnp.dot(normed, full_key, preferred_element_type=jnp.float32), position, 1.0
    ).astype(jnp.bfloat16)
    values_local = jnp.dot(normed, full_value, preferred_element_type=jnp.float32).astype(
        jnp.bfloat16
    )
    all_keys, all_values = (
        lax.all_gather(keys_local, "ctx", axis=0, tiled=True),
        lax.all_gather(values_local, "ctx", axis=0, tiled=True),
    )
    key_block = math.gcd(group_rows, 512)
    block_count = group_rows // key_block
    blocks_in = (
        all_keys.reshape(block_count, key_block, head_count, HEAD),
        all_values.reshape(block_count, key_block, head_count, HEAD),
        key_valid.reshape(block_count, key_block),
        key_slot.reshape(block_count, key_block),
        key_index.reshape(block_count, key_block),
    )
    query_heads = queries.reshape(local_rows, head_count, HEAD)

    def mask_of(inputs):
        key_ids = inputs[4]
        return (
            query_valid[:, None]
            & inputs[2][None, :]
            & (key_ids[None, :] <= query_index[:, None])
            & ((key_ids[None, :] < prompt) | (inputs[3][None, :] == query_slot[:, None]))
        )

    def raw_scores(inputs):
        return (
            jnp.einsum("qhd,khd->hqk", query_heads, inputs[0], preferred_element_type=jnp.float32)
            * score_scale
        )

    def running(state_in, inputs):
        allowed = mask_of(inputs)

        def running_visit(state):
            row_top, exp_total = state
            scores = jnp.where(allowed[None], raw_scores(inputs), masked_out)
            new_top = jnp.maximum(row_top, jnp.max(scores, axis=-1, keepdims=True))
            exp_total = exp_total * jnp.exp(row_top - new_top) + jnp.sum(
                jnp.where(allowed[None], jnp.exp(scores - new_top), 0.0), axis=-1, keepdims=True
            )
            return (new_top, exp_total)

        return (lax.cond(jnp.any(allowed), running_visit, keep_same, state_in), None)

    start_top = jnp.full((head_count, local_rows, 1), -jnp.inf, jnp.float32)
    start_total = jnp.zeros((head_count, local_rows, 1), jnp.float32)
    (row_top, exp_total), unused = lax.scan(running, (start_top, start_total), blocks_in)
    has_keys = exp_total > 0.0
    log_total = jnp.where(has_keys, row_top + jnp.log(jnp.where(has_keys, exp_total, 1.0)), 0.0)

    def probs_of(inputs, allowed):
        return jnp.where(allowed[None], jnp.exp(raw_scores(inputs) - log_total), 0.0)

    def mix_step(accumulated, inputs):
        allowed = mask_of(inputs)

        def mix_visit(total):
            attn_probs = probs_of(inputs, allowed).astype(jnp.bfloat16)
            return total + jnp.einsum(
                "hqk,khd->qhd", attn_probs, inputs[1], preferred_element_type=jnp.float32
            )

        return (lax.cond(jnp.any(allowed), mix_visit, keep_same, accumulated), None)

    mixture, unused = lax.scan(
        mix_step, jnp.zeros((local_rows, head_count, HEAD), jnp.float32), blocks_in
    )
    valid_col = query_valid[:, None].astype(jnp.float32)
    attended = (mixture.reshape(local_rows, model_width) * valid_col).astype(jnp.bfloat16)
    branch = jnp.dot(attended, full_out, preferred_element_type=jnp.float32)
    branch_normed, inverse_two = rms_norm(branch, norm_two)
    middle = tokens + branch_normed
    full_gate, full_up, full_down = (
        lax.all_gather(w_gate, "fsdp", axis=0, tiled=True),
        lax.all_gather(w_up, "fsdp", axis=0, tiled=True),
        lax.all_gather(w_down, "fsdp", axis=0, tiled=True),
    )
    ff_normed, inverse_three = rms_norm(middle, norm_three)
    ff_input = ff_normed.astype(jnp.bfloat16)
    gate_pre = jnp.dot(ff_input, full_gate, preferred_element_type=jnp.float32)
    upward = jnp.dot(ff_input, full_up, preferred_element_type=jnp.float32)
    gate_sig = jax.nn.sigmoid(gate_pre)
    swish_out = gate_pre * gate_sig
    hidden = (swish_out * upward).astype(jnp.bfloat16)
    ff_out = jnp.dot(hidden, full_down, preferred_element_type=jnp.float32)
    out_normed, inverse_four = rms_norm(ff_out, norm_four)
    result = middle + out_normed
    upstream = out_grad[0].astype(jnp.float32)
    ff_out_full, grad_norm_four = norm_back(ff_out, inverse_four, norm_four, upstream)
    ff_out_grad = ff_out_full.astype(jnp.bfloat16)
    hidden_grad = back_dot(ff_out_grad, full_down)
    up_grad = (hidden_grad * swish_out).astype(jnp.bfloat16)
    gate_grad = (hidden_grad * upward * gate_sig * (1.0 + gate_pre * (1.0 - gate_sig))).astype(
        jnp.bfloat16
    )
    ff_in_grad = back_dot(gate_grad, full_gate) + back_dot(up_grad, full_up)
    middle_part, grad_norm_three = norm_back(middle, inverse_three, norm_three, ff_in_grad)
    middle_grad = upstream + middle_part
    branch_full, grad_norm_two = norm_back(branch, inverse_two, norm_two, middle_grad)
    branch_grad = branch_full.astype(jnp.bfloat16)
    attended_grad = back_dot(branch_grad, full_out).astype(jnp.bfloat16) * valid_col.astype(
        jnp.bfloat16
    )
    grad_heads = attended_grad.reshape(local_rows, head_count, HEAD)

    def delta_step(accumulated, inputs):
        allowed = mask_of(inputs)

        def delta_visit(total):
            attn_probs = probs_of(inputs, allowed)
            prob_grad = jnp.einsum(
                "qhd,khd->hqk", grad_heads, inputs[1], preferred_element_type=jnp.float32
            )
            return total + jnp.sum(attn_probs * prob_grad, axis=-1, keepdims=True)

        return (lax.cond(jnp.any(allowed), delta_visit, keep_same, accumulated), None)

    row_delta, unused = lax.scan(
        delta_step, jnp.zeros((head_count, local_rows, 1), jnp.float32), blocks_in
    )
    zero_part = jnp.zeros((key_block, head_count, HEAD), jnp.float32)

    def grad_step(accumulated, inputs):
        allowed = mask_of(inputs)

        def grad_visit(total):
            attn_probs = probs_of(inputs, allowed)
            prob_grad = jnp.einsum(
                "qhd,khd->hqk", grad_heads, inputs[1], preferred_element_type=jnp.float32
            )
            score_grad = (attn_probs * (prob_grad - row_delta)).astype(jnp.bfloat16)
            total = total + jnp.einsum(
                "hqk,khd->qhd", score_grad, inputs[0], preferred_element_type=jnp.float32
            )
            key_part = jnp.einsum(
                "hqk,qhd->khd", score_grad, query_heads, preferred_element_type=jnp.float32
            )
            value_part = jnp.einsum(
                "hqk,qhd->khd",
                attn_probs.astype(jnp.bfloat16),
                grad_heads,
                preferred_element_type=jnp.float32,
            )
            return (total, (key_part, value_part))

        def skip(total):
            return (total, (zero_part, zero_part))

        return lax.cond(jnp.any(allowed), grad_visit, skip, accumulated)

    query_acc, (key_parts, value_parts) = lax.scan(
        grad_step, jnp.zeros((local_rows, head_count, HEAD), jnp.float32), blocks_in
    )
    key_terms = key_parts.reshape(group_rows, model_width) * score_scale
    value_terms = value_parts.reshape(group_rows, model_width)
    key_sum, value_sum = (
        lax.psum_scatter(
            key_terms.astype(jnp.bfloat16), "ctx", scatter_dimension=0, tiled=True
        ).astype(jnp.float32),
        lax.psum_scatter(
            value_terms.astype(jnp.bfloat16), "ctx", scatter_dimension=0, tiled=True
        ).astype(jnp.float32),
    )
    query_grad = rotate(
        query_acc.reshape(local_rows, model_width) * score_scale, position, -1.0
    ).astype(jnp.bfloat16)
    key_grad = rotate(key_sum, position, -1.0).astype(jnp.bfloat16)
    value_grad = value_sum.astype(jnp.bfloat16)
    normed_grad = (
        back_dot(query_grad, full_query)
        + back_dot(key_grad, full_key)
        + back_dot(value_grad, full_value)
    )
    input_part, grad_norm_one = norm_back(tokens, inverse_one, norm_one, normed_grad)
    input_grad = middle_grad + input_part
    wide_pairs = (
        (normed, query_grad),
        (normed, key_grad),
        (normed, value_grad),
        (attended, branch_grad),
        (ff_input, gate_grad),
        (ff_input, up_grad),
    )

    def wide_term(selector):
        return jnp.concatenate(
            [cross_dot(selector(operand), partner) for operand, partner in wide_pairs], axis=1
        )

    wide_local = lax.psum_scatter(
        wide_term(lambda operand: operand).astype(jnp.bfloat16),
        "fsdp",
        scatter_dimension=0,
        tiled=True,
    )
    ff_local = lax.psum_scatter(
        cross_dot((lambda operand: operand)(hidden), ff_out_grad).astype(jnp.bfloat16),
        "fsdp",
        scatter_dimension=0,
        tiled=True,
    )
    wide_sum, ff_sum = (
        lax.psum(wide_local, "ctx").astype(jnp.float32),
        lax.psum(ff_local, "ctx").astype(jnp.float32),
    )
    gain_sums = lax.psum(
        jnp.stack([grad_norm_one, grad_norm_two, grad_norm_three, grad_norm_four]), ("ctx", "fsdp")
    )
    edge_two = 2 * model_width
    edge_three = 3 * model_width
    edge_four = 4 * model_width
    edge_five = 4 * model_width + ff_width
    return (
        result.astype(jnp.bfloat16)[None],
        input_grad[None],
        wide_sum[:, :model_width],
        wide_sum[:, model_width:edge_two],
        wide_sum[:, edge_two:edge_three],
        wide_sum[:, edge_three:edge_four],
        gain_sums[0],
        gain_sums[1],
        wide_sum[:, edge_four:edge_five],
        wide_sum[:, edge_five:],
        ff_sum,
        gain_sums[2],
        gain_sums[3],
    )


def solution(mesh):
    return jax.shard_map(
        shards,
        mesh=mesh,
        in_specs=(
            P("fsdp", "ctx", None),
            P("fsdp", "ctx", None),
            P("fsdp", None),
            P("fsdp", None),
            P("fsdp", None),
            P("fsdp", None),
            P(),
            P(),
            P("fsdp", None),
            P("fsdp", None),
            P("fsdp", None),
            P(),
            P(),
            P(),
            P(),
            P(),
            P(),
        ),
        out_specs=(
            P("fsdp", "ctx", None),
            P("fsdp", "ctx", None),
            P("fsdp", None),
            P("fsdp", None),
            P("fsdp", None),
            P("fsdp", None),
            P(),
            P(),
            P("fsdp", None),
            P("fsdp", None),
            P("fsdp", None),
            P(),
            P(),
        ),
        check_vma=False,
    )
```

profile of v0, /device:TPU:0, one launch (start us, length us, event | category | flops | bytes accessed | tf_op | source)
XLA Modules:
  0.0 1122.9 jit_solution(17604052558741267211)
XLA Ops:
  16.3 18.6 %all-gather.14.cloned.1.call-done = bf16[1024,1024]{1,0:T(8,128)(2,1)} async-done(((bf16[256,1024]{1,0:T(8,128)(2,1)}), bf16[1024,1024]{1,0:T(8,128)(2,1)}) %all-gather.14.cloned.1.call-update) | async-done | bytes 2097168 | tf_op jit(solution)/shard_map/all_gather | solution.py:114
  37.8 21.3 %all-gather.10.cloned.1.call-done = bf16[1024,1024]{1,0:T(8,128)(2,1)} async-done(((bf16[256,1024]{1,0:T(8,128)(2,1)}), bf16[1024,1024]{1,0:T(8,128)(2,1)}) %all-gather.10.cloned.1.call-update) | async-done | bytes 2097168 | tf_op jit(solution)/shard_map/all_gather | solution.py:115
  59.1 3.9 copy.83
  67.9 15.3 %all-gather.16.cloned.1.call-done = bf16[1024,1024]{1,0:T(8,128)(2,1)} async-done(((bf16[256,1024]{1,0:T(8,128)(2,1)}), bf16[1024,1024]{1,0:T(8,128)(2,1)}) %all-gather.16.cloned.1.call-update) | async-done | bytes 2097168 | tf_op jit(solution)/shard_map/all_gather | solution.py:116
  92.4 66.9 %all-gather.12.cloned.1.call-done = bf16[2048,1024]{1,0:T(8,128)(2,1)} async-done(((bf16[256,1024]{1,0:T(8,128)(2,1)}), bf16[2048,1024]{1,0:T(8,128)(2,1)}) %all-gather.12.cloned.1.call-update) | async-done | bytes 4194320 | tf_op jit(solution)/shard_map/all_gather | solution.py:131
  165.5 68.0 %all-gather.18.cloned.1.call-done = bf16[2048,1024]{1,0:T(8,128)(2,1)} async-done(((bf16[256,1024]{1,0:T(8,128)(2,1)}), bf16[2048,1024]{1,0:T(8,128)(2,1)}) %all-gather.18.cloned.1.call-update) | async-done | bytes 4194320 | tf_op jit(solution)/shard_map/all_gather | solution.py:132
  239.7 10.0 while.63
  249.8 10.7 while.64
  267.4 33.4 %all-gather.22.cloned.1.call-done = bf16[1024,2816]{1,0:T(8,128)(2,1)} async-done(((bf16[256,2816]{1,0:T(8,128)(2,1)}), bf16[1024,2816]{1,0:T(8,128)(2,1)}) %all-gather.22.cloned.1.call-update) | async-done | bytes 5767184 | tf_op jit(solution)/shard_map/all_gather | solution.py:203
  300.8 6.0 fusion.145
  306.8 39.0 %all-gather.24.cloned.1.call-done = bf16[1024,2816]{1,0:T(8,128)(2,1)} async-done(((bf16[256,2816]{1,0:T(8,128)(2,1)}), bf16[1024,2816]{1,0:T(8,128)(2,1)}) %all-gather.24.cloned.1.call-update) | async-done | bytes 5767184 | tf_op jit(solution)/shard_map/all_gather | solution.py:204
  345.8 7.4 multiply_convert_fusion.3
  353.2 37.6 %all-gather.26.cloned.1.call-done = bf16[2816,1024]{1,0:T(8,128)(2,1)} async-done(((bf16[704,1024]{1,0:T(8,128)(2,1)}), bf16[2816,1024]{1,0:T(8,128)(2,1)}) %all-gather.26.cloned.1.call-update) | async-done | bytes 5767184 | tf_op jit(solution)/shard_map/all_gather | solution.py:205
  390.8 5.0 multiply_reduce_fusion.4
  398.1 6.0 multiply_convert_fusion.1
  410.5 11.4 %while.65 = (s32[]{:T(128)}, f32[8,256,1]{1,2,0:T(1,128)S(1)}, pred[256]{0:T(512)(128)(4,1)S(1)}, pred[4,512]{1,0:T(4,128)(4,1)S(1)}, s32[4,512]{1,0:T(4,128)S(1...) while((s32[]{:T(128)}, f32[8,256,1]{1,2,0:T(1,128)S(1)}, ...), condition=%wide.region_31.32_spmd.clone.clone, body=%wide.region_26.31_spmd.clone.clone.sunk | while | flops 543035136 | bytes 11857887 | solution.py:247
  412.2 4.5 conditional.18
  423.0 38.1 %while.66 = (s32[]{:T(128)}, f32[256,8,128]{2,0,1:T(8,128)}, f32[4,512,8,128]{3,1,2,0:T(8,128)}, bf16[4,512,8,128]{3,1,2,0:T(8,128)(2,1)}, pred[256]{0:T(512)(12...) while((s32[]{:T(128)}, f32[256,8,128]{2,0,1:T(8,128)}, ...), condition=%wide.region_36.37_spmd.clone.clone, body=%wide.region_32.36_spmd.clone.clone.sunk | while | flops 1353846528 | bytes 89568512 | solution.py:280
  424.6 9.4 conditional.19
  461.1 4.6 multiply_convert_fusion
  471.7 4.9 copy.108
  481.1 4.2 convolution_convert_fusion
  491.1 4.2 copy.112
  496.4 90.5 %reduce-scatter.5.cloned.1.call-done = bf16[256,1024]{1,0:T(8,128)(2,1)} async-done(((bf16[2048,1024]{1,0:T(8,128)(2,1)}), bf16[256,1024]{1,0:T(8,128)(2,1)}) %reduce-scatter.5.cloned.1.call-update) | async-done | bytes 524304 | tf_op jit(solution)/shard_map/reduce_scatter | solution.py:286
  601.1 3.9 copy.110
  605.0 73.9 %reduce-scatter.7.cloned.1.call-done = bf16[256,1024]{1,0:T(8,128)(2,1)} async-done(((bf16[2048,1024]{1,0:T(8,128)(2,1)}), bf16[256,1024]{1,0:T(8,128)(2,1)}) %reduce-scatter.7.cloned.1.call-update) | async-done | bytes 524304 | tf_op jit(solution)/shard_map/reduce_scatter | solution.py:289
  693.5 4.2 convert_dynamic-update-slice_fusion.1
  697.7 4.5 convert_dynamic-update-slice_fusion
  702.2 33.7 %reduce-scatter.11.cloned.1.call-done = bf16[704,1024]{1,0:T(8,128)(2,1)} async-done(((bf16[2816,1024]{1,0:T(8,128)(2,1)}), bf16[704,1024]{1,0:T(8,128)(2,1)}) %reduce-scatter.11.cloned.1.call-update) | async-done | bytes 1441808 | tf_op jit(solution)/shard_map/reduce_scatter | solution.py:325
  735.9 149.1 %reduce-scatter.9.cloned.1.call-done = bf16[256,9728]{1,0:T(8,128)(2,1)} async-done(((bf16[1024,9728]{1,0:T(8,128)(2,1)}), bf16[256,9728]{1,0:T(8,128)(2,1)}) %reduce-scatter.9.cloned.1.call-update) | async-done | bytes 4980752 | tf_op jit(solution)/shard_map/reduce_scatter | solution.py:319
  889.7 43.4 %psum.22 = f32[4,1024]{1,0:T(4,128)S(1)} all-reduce(f32[4,1024]{1,0:T(4,128)S(1)} %pad_maximum_fusion.2), channel_id=1, replica_groups=mesh['ctx'=8,'fsdp'=4] {'ctx','fsdp'}, use_global_device_ids=true, to_apply=%region_46.47 | all-reduce | flops 4096 | bytes 32768 | tf_op jit(solution)/shard_map/psum | solution.py:335
  935.0 172.4 %all-reduce.3.cloned.1.call-done = (bf16[256,9728]{1,0:T(8,128)(2,1)}, bf16[704,1024]{1,0:T(8,128)(2,1)}) async-done(((bf16[256,9728]{1,0:T(8,128)(2,1)}, bf16[704,1024]{1,0:T(8,128)(2,1)}), (bf16[256,9728]{1,0:T(8,128)(2,1)}, bf16[704,1024]{1,0:T(8,128)(2,1)})) %all-reduce.3.cloned.1.call-update) | async-done | bytes 6422544 | tf_op jit(solution)/shard_map/psum | solution.py:332
  (366 shorter events, 182.4 us)
Async XLA Ops:
  7.2 27.7 %all-gather.14.cloned.1.call-start = ((), (), s32[]{:S(2)}) async-start(), calls=%async_computation.6 | async-start | bytes 2621440 | tf_op jit(solution)/shard_map/all_gather | solution.py:114
  7.9 51.2 %all-gather.10.cloned.1.call-start = ((), (), s32[]{:S(2)}) async-start(), calls=%async_computation.4 | async-start | bytes 2621440 | tf_op jit(solution)/shard_map/all_gather | solution.py:115
  8.7 74.6 %all-gather.16.cloned.1.call-start = ((), (), s32[]{:S(2)}) async-start(), calls=%async_computation.7 | async-start | bytes 2621440 | tf_op jit(solution)/shard_map/all_gather | solution.py:116
  9.4 149.9 %all-gather.12.cloned.1.call-start = ((), (), s32[]{:S(2)}) async-start(), calls=%async_computation.5 | async-start | bytes 4718592 | tf_op jit(solution)/shard_map/all_gather | solution.py:131
  15.0 51.4 %copy-start.26 = (f32[256,128]{0,1:T(8,128)}, f32[256,128]{0,1:T(8,128)S(1)}, u32[]{:S(2)}) copy-start(f32[256,128]{0,1:T(8,128)S(1)} %get-tuple-element.1103) | copy-start | bytes 393220
  16.3 67.0 %copy-start.37 = (f32[256]{0:T(256)}, f32[256]{0:T(256)S(1)}, u32[]{:S(2)}) copy-start(f32[256]{0:T(256)S(1)} %add_rsqrt_fusion.3) | copy-start | bytes 3076
  34.9 28.1 %copy-start.3 = (bf16[1,256,1024]{2,1,0:T(8,128)(2,1)S(1)}, bf16[1,256,1024]{2,1,0:T(8,128)(2,1)}, u32[]{:S(2)}) copy-start(bf16[1,256,1024]{2,1,0:T(8,128)(2,1)} %param.33) | copy-start | bytes 1572868
  34.9 28.1 %copy-start.35 = (f32[1024]{0:T(1024)S(1)}, f32[1024]{0:T(1024)}, u32[]{:S(2)}) copy-start(f32[1024]{0:T(1024)} %param.39) | copy-start | bytes 12292
  67.9 22.3 %copy-start.43 = (s32[4,2]{0,1:T(2,128)S(1)}, s32[4,2]{0,1:T(2,128)}, u32[]{:S(2)}) copy-start(s32[4,2]{0,1:T(2,128)} %param.47) | copy-start | bytes 100
  67.9 22.3 %copy-start.44 = (s32[4,2]{0,1:T(2,128)S(1)}, s32[4,2]{0,1:T(2,128)}, u32[]{:S(2)}) copy-start(s32[4,2]{0,1:T(2,128)} %param.49) | copy-start | bytes 100
  67.9 165.6 %all-gather.18.cloned.1.call-start = ((), (), s32[]{:S(2)}) async-start(), calls=%async_computation.8 | async-start | bytes 4718592 | tf_op jit(solution)/shard_map/all_gather | solution.py:132
  86.4 176.7 %all-gather.20.cloned.1.call-start = ((), (), s32[]{:S(2)}) async-start(), calls=%async_computation.9 | async-start | bytes 2621440 | tf_op jit(solution)/shard_map/all_gather | solution.py:117
  87.0 213.8 %all-gather.22.cloned.1.call-start = ((), (), s32[]{:S(2)}) async-start(), calls=%async_computation.10 | async-start | bytes 7208960 | tf_op jit(solution)/shard_map/all_gather | solution.py:203
  87.8 258.0 %all-gather.24.cloned.1.call-start = ((), (), s32[]{:S(2)}) async-start(), calls=%async_computation.11 | async-start | bytes 7208960 | tf_op jit(solution)/shard_map/all_gather | solution.py:204
  88.5 302.3 %all-gather.26.cloned.1.call-start = ((), (), s32[]{:S(2)}) async-start(), calls=%async_computation.12 | async-start | bytes 7208960 | tf_op jit(solution)/shard_map/all_gather | solution.py:205
  89.3 497.7 %reduce-scatter.5.cloned.1.call-start = ((), (), s32[]{:S(2)}) async-start(), calls=%async_computation.13 | async-start | bytes 4718592 | tf_op jit(solution)/shard_map/reduce_scatter | solution.py:286
  260.5 5.5 copy-start.39
  390.8 7.3 slice-start.4
  390.8 7.3 slice-start.5
  396.8 7.4 slice-start
  396.8 9.1 slice-start.2
  398.1 6.1 copy-start.23
  398.1 6.1 slice-start.1
  398.1 7.8 slice-start.3
  471.6 207.3 %reduce-scatter.7.cloned.1.call-start = ((), (), s32[]{:S(2)}) async-start(), calls=%async_computation.14 | async-start | bytes 4718592 | tf_op jit(solution)/shard_map/reduce_scatter | solution.py:289
  479.6 256.3 %reduce-scatter.11.cloned.1.call-start = ((), (), s32[]{:S(2)}) async-start(), calls=%async_computation.16 | async-start | bytes 7208960 | tf_op jit(solution)/shard_map/reduce_scatter | solution.py:325
  485.3 399.7 %reduce-scatter.9.cloned.1.call-start = ((), (), s32[]{:S(2)}) async-start(), calls=%async_computation.15 | async-start | bytes 24903680 | tf_op jit(solution)/shard_map/reduce_scatter | solution.py:319
  495.2 93.1 %copy-start.28 = (f32[256,128]{0,1:T(8,128)S(1)}, f32[256,128]{0,1:T(8,128)}, u32[]{:S(2)}) copy-start(f32[256,128]{0,1:T(8,128)} %get-tuple-element.1104) | copy-start | bytes 393220
  495.2 93.1 %copy-start.29 = (f32[256,128]{0,1:T(8,128)S(1)}, f32[256,128]{0,1:T(8,128)}, u32[]{:S(2)}) copy-start(f32[256,128]{0,1:T(8,128)} %get-tuple-element.1102) | copy-start | bytes 393220
  702.2 182.9 %copy-start.7 = (bf16[1024,1024]{1,0:T(8,128)(2,1)S(1)}, bf16[1024,1024]{1,0:T(8,128)(2,1)}, u32[]{:S(2)}) copy-start(bf16[1024,1024]{1,0:T(8,128)(2,1)} %all-gather.14.cloned.1.call-done) | copy-start | bytes 6291460
  702.2 405.2 %all-reduce.3.cloned.1.call-start = ((), (), s32[]{:S(2)}) async-start(), calls=%async_computation.17 | async-start | bytes 12845056 | tf_op jit(solution)/shard_map/psum | solution.py:332
  886.7 47.0 %copy-start.6 = (f32[256,1024]{1,0:T(8,128)S(1)}, f32[256,1024]{1,0:T(8,128)}, u32[]{:S(2)}) copy-start(f32[256,1024]{1,0:T(8,128)} %copy-done.5) | copy-start | bytes 3145732
  (49 other events, 131.7 us)
Sparse Core Ops, SparseCore 0:
  9.6 25.2 all-gather.13
  36.5 22.5 all-gather.9
  60.6 22.5 all-gather.15
  85.8 73.3 all-gather.11
  161.8 71.6 all-gather.17
  234.9 20.8 all-gather.19
  257.4 43.3 all-gather.21
  302.4 43.3 all-gather.23
  347.4 43.3 all-gather.25
  471.7 115.1 reduce-scatter.4
  591.0 87.8 reduce-scatter.6
  681.3 54.5 reduce-scatter.10
  738.7 146.2 reduce-scatter.8
  888.9 218.4 all-reduce.2
where the time goes:
time: 1130 us; the launch traced here: 1120 us
  waiting for transfers between devices  824 us (73%)
  local copies, waits for them, and re-layouts  97.8 us (9%)
  matrix products  83.8 us (7%)
  other arithmetic  46.4 us (4%)
  blocking collectives  43.4 us (4%)
  between operations  15 us (1%)
  loops' own time  11.6 us (1%)
    psum x1, waiting for transfers between devices, shards(): lax.psum(wide_local, 'ctx').astype(jnp.float32)  172 us
    reduce_scatter x1, waiting for transfers between devices, shards(): lax.psum_scatter(wide_term(lambda operand: operand).astype(jnp.bfloat16),...  149 us
    reduce_scatter x1, waiting for transfers between devices, shards(): lax.psum_scatter(key_terms.astype(jnp.bfloat16), 'ctx', scatter_dimension...  90.5 us
    reduce_scatter x1, waiting for transfers between devices, shards(): lax.psum_scatter(value_terms.astype(jnp.bfloat16), 'ctx', scatter_dimensi...  73.9 us
    all_gather x1, waiting for transfers between devices, shards(): lax.all_gather(values_local, 'ctx', axis=0, tiled=True)  68 us
    all_gather x1, waiting for transfers between devices, shards(): lax.all_gather(keys_local, 'ctx', axis=0, tiled=True)  66.9 us
    psum x1, blocking collectives, shards(): lax.psum(jnp.stack([grad_norm_one, grad_norm_two, grad_norm_three, grad_n...  43.4 us
    all_gather x1, waiting for transfers between devices, shards(): lax.all_gather(w_up, 'fsdp', axis=0, tiled=True)  39 us
  transfers between devices with their start and end apart: 14, of which 13 were waited for; matrix products, arithmetic and copies ran while one was open for 12% of the time, Pallas kernels for 0%

commit v1 on v0

--- a/solution.py
+++ b/solution.py
@@ -329,7 +329,7 @@
         tiled=True,
     )
     wide_sum, ff_sum = (
-        lax.psum(wide_local, "ctx").astype(jnp.float32),
+        jnp.sum(lax.all_gather(wide_local, "ctx"), axis=0).astype(jnp.float32),
         lax.psum(ff_local, "ctx").astype(jnp.float32),
     )
     gain_sums = lax.psum(

time: 1130 us -> 1770 us (1.57)
  waiting for transfers between devices: 824 us -> 1450 us
  other arithmetic: 46.4 us -> 64.3 us
    all_gather x0 -> x1, waiting for transfers between devices: none -> 753 us  [shards(): lax.all_gather(wide_local, 'ctx')]
    psum x1, waiting for transfers between devices: 172 us -> 42.9 us  [shards(): lax.psum(ff_local, 'ctx').astype(jnp.float32)]
  transfers between devices with their start and end apart: 14 -> 15, of which waited for: 13 -> 14; matrix products, arithmetic and copies ran while one was open for 12% -> 8% of each run, Pallas kernels for 0% -> 0%
where the time goes in v1:
time: 1770 us; the launch traced here: 1760 us
  waiting for transfers between devices  1450 us (82%)
  local copies, waits for them, and re-layouts  97.8 us (6%)
  matrix products  83.8 us (5%)
  other arithmetic  64.3 us (4%)
  blocking collectives  40.9 us (2%)
    all_gather x1, waiting for transfers between devices, shards(): lax.all_gather(wide_local, 'ctx')  753 us
    reduce_scatter x1, waiting for transfers between devices, shards(): lax.psum_scatter(wide_term(lambda operand: operand).astype(jnp.bfloat16),...  149 us
    reduce_scatter x1, waiting for transfers between devices, shards(): lax.psum_scatter(key_terms.astype(jnp.bfloat16), 'ctx', scatter_dimension...  90.5 us
    reduce_scatter x1, waiting for transfers between devices, shards(): lax.psum_scatter(value_terms.astype(jnp.bfloat16), 'ctx', scatter_dimensi...  73.7 us
    all_gather x1, waiting for transfers between devices, shards(): lax.all_gather(values_local, 'ctx', axis=0, tiled=True)  68 us
    all_gather x1, waiting for transfers between devices, shards(): lax.all_gather(keys_local, 'ctx', axis=0, tiled=True)  66.9 us
    psum x1, waiting for transfers between devices, shards(): lax.psum(ff_local, 'ctx').astype(jnp.float32)  42.9 us
    psum x1, blocking collectives, shards(): lax.psum(jnp.stack([grad_norm_one, grad_norm_two, grad_norm_three, grad_n...  40.9 us
  transfers between devices with their start and end apart: 15, of which 14 were waited for; matrix products, arithmetic and copies ran while one was open for 8% of the time, Pallas kernels for 0%

profile of v1, /device:TPU:0, one launch (start us, length us, event | category | flops | bytes accessed | tf_op | source)
XLA Modules:
  0.0 1762.0 jit_solution(17170568376648721349)
XLA Ops:
  16.3 18.6 %all-gather.16.cloned.1.call-done = bf16[1024,1024]{1,0:T(8,128)(2,1)} async-done(((bf16[256,1024]{1,0:T(8,128)(2,1)}), bf16[1024,1024]{1,0:T(8,128)(2,1)}) %all-gather.16.cloned.1.call-update) | async-done | bytes 2097168 | tf_op jit(solution)/shard_map/all_gather | solution.py:114
  37.8 21.3 %all-gather.12.cloned.1.call-done = bf16[1024,1024]{1,0:T(8,128)(2,1)} async-done(((bf16[256,1024]{1,0:T(8,128)(2,1)}), bf16[1024,1024]{1,0:T(8,128)(2,1)}) %all-gather.12.cloned.1.call-update) | async-done | bytes 2097168 | tf_op jit(solution)/shard_map/all_gather | solution.py:115
  67.9 15.3 all-gather.18.cloned.1.call-done
  92.4 66.9 %all-gather.14.cloned.1.call-done = bf16[2048,1024]{1,0:T(8,128)(2,1)} async-done(((bf16[256,1024]{1,0:T(8,128)(2,1)}), bf16[2048,1024]{1,0:T(8,128)(2,1)}) %all-gather.14.cloned.1.call-update) | async-done | bytes 4194320 | tf_op jit(solution)/shard_map/all_gather | solution.py:131
  165.5 68.0 %all-gather.20.cloned.1.call-done = bf16[2048,1024]{1,0:T(8,128)(2,1)} async-done(((bf16[256,1024]{1,0:T(8,128)(2,1)}), bf16[2048,1024]{1,0:T(8,128)(2,1)}) %all-gather.20.cloned.1.call-update) | async-done | bytes 4194320 | tf_op jit(solution)/shard_map/all_gather | solution.py:132
  239.6 10.0 while.63
  249.7 10.7 while.64
  267.4 33.4 %all-gather.24.cloned.1.call-done = bf16[1024,2816]{1,0:T(8,128)(2,1)} async-done(((bf16[256,2816]{1,0:T(8,128)(2,1)}), bf16[1024,2816]{1,0:T(8,128)(2,1)}) %all-gather.24.cloned.1.call-update) | async-done | bytes 5767184 | tf_op jit(solution)/shard_map/all_gather | solution.py:203
  300.8 6.0 fusion.145
  306.8 39.0 %all-gather.26.cloned.1.call-done = bf16[1024,2816]{1,0:T(8,128)(2,1)} async-done(((bf16[256,2816]{1,0:T(8,128)(2,1)}), bf16[1024,2816]{1,0:T(8,128)(2,1)}) %all-gather.26.cloned.1.call-update) | async-done | bytes 5767184 | tf_op jit(solution)/shard_map/all_gather | solution.py:204
  345.8 7.4 multiply_convert_fusion.3
  353.2 37.6 %all-gather.28.cloned.1.call-done = bf16[2816,1024]{1,0:T(8,128)(2,1)} async-done(((bf16[704,1024]{1,0:T(8,128)(2,1)}), bf16[2816,1024]{1,0:T(8,128)(2,1)}) %all-gather.28.cloned.1.call-update) | async-done | bytes 5767184 | tf_op jit(solution)/shard_map/all_gather | solution.py:205
  390.8 5.0 multiply_reduce_fusion.4
  398.1 6.1 multiply_convert_fusion.1
  410.5 11.4 while.65
  412.2 4.5 conditional.18
  423.0 38.2 %while.66 = (s32[]{:T(128)}, f32[256,8,128]{2,0,1:T(8,128)}, f32[4,512,8,128]{3,1,2,0:T(8,128)}, bf16[4,512,8,128]{3,1,2,0:T(8,128)(2,1)}, pred[256]{0:T(512)(12...) while((s32[]{:T(128)}, f32[256,8,128]{2,0,1:T(8,128)}, ...), condition=%wide.region_36.37_spmd.clone.clone, body=%wide.region_32.36_spmd.clone.clone.sunk | while | flops 1353846528 | bytes 89568512 | solution.py:280
  424.7 9.5 conditional.19
  461.2 4.6 multiply_convert_fusion
  471.7 4.9 copy.108
  481.1 4.2 convolution_convert_fusion
  491.1 4.1 copy.112
  496.4 90.5 %reduce-scatter.5.cloned.1.call-done = bf16[256,1024]{1,0:T(8,128)(2,1)} async-done(((bf16[2048,1024]{1,0:T(8,128)(2,1)}), bf16[256,1024]{1,0:T(8,128)(2,1)}) %reduce-scatter.5.cloned.1.call-update) | async-done | bytes 524304 | tf_op jit(solution)/shard_map/reduce_scatter | solution.py:286
  605.0 73.7 %reduce-scatter.7.cloned.1.call-done = bf16[256,1024]{1,0:T(8,128)(2,1)} async-done(((bf16[2048,1024]{1,0:T(8,128)(2,1)}), bf16[256,1024]{1,0:T(8,128)(2,1)}) %reduce-scatter.7.cloned.1.call-update) | async-done | bytes 524304 | tf_op jit(solution)/shard_map/reduce_scatter | solution.py:289
  693.3 4.2 convert_dynamic-update-slice_fusion.1
  697.5 4.5 convert_dynamic-update-slice_fusion
  702.1 33.7 %reduce-scatter.11.cloned.1.call-done = bf16[704,1024]{1,0:T(8,128)(2,1)} async-done(((bf16[2816,1024]{1,0:T(8,128)(2,1)}), bf16[704,1024]{1,0:T(8,128)(2,1)}) %reduce-scatter.11.cloned.1.call-update) | async-done | bytes 1441808 | tf_op jit(solution)/shard_map/reduce_scatter | solution.py:325
  735.8 149.0 %reduce-scatter.9.cloned.1.call-done = bf16[256,9728]{1,0:T(8,128)(2,1)} async-done(((bf16[1024,9728]{1,0:T(8,128)(2,1)}), bf16[256,9728]{1,0:T(8,128)(2,1)}) %reduce-scatter.9.cloned.1.call-update) | async-done | bytes 4980752 | tf_op jit(solution)/shard_map/reduce_scatter | solution.py:319
  889.6 40.9 %psum.14 = f32[4,1024]{1,0:T(4,128)S(1)} all-reduce(f32[4,1024]{1,0:T(4,128)S(1)} %pad_maximum_fusion.2), channel_id=1, replica_groups=mesh['ctx'=8,'fsdp'=4] {'ctx','fsdp'}, use_global_device_ids=true, to_apply=%region_46.47 | all-reduce | flops 4096 | bytes 32768 | tf_op jit(solution)/shard_map/psum | solution.py:335
  932.4 42.9 %all-reduce.2.cloned.1.call-done = bf16[704,1024]{1,0:T(8,128)(2,1)} async-done(((bf16[704,1024]{1,0:T(8,128)(2,1)}), bf16[704,1024]{1,0:T(8,128)(2,1)}) %all-reduce.2.cloned.1.call-update) | async-done | bytes 1441808 | tf_op jit(solution)/shard_map/psum | solution.py:333
  978.6 753.2 %all-gather.30.cloned.1.call-done = bf16[2048,9728]{1,0:T(8,128)(2,1)} async-done(((bf16[256,9728]{1,0:T(8,128)(2,1)}), bf16[2048,9728]{1,0:T(8,128)(2,1)}) %all-gather.30.cloned.1.call-update) | async-done | bytes 39845904 | tf_op jit(solution)/shard_map/all_gather | solution.py:332
  1731.8 16.6 reduce_sum.222
  (368 shorter events, 191.7 us)
Async XLA Ops:
  7.2 27.7 %all-gather.16.cloned.1.call-start = ((), (), s32[]{:S(2)}) async-start(), calls=%async_computation.6 | async-start | bytes 2621440 | tf_op jit(solution)/shard_map/all_gather | solution.py:114
  7.9 51.2 %all-gather.12.cloned.1.call-start = ((), (), s32[]{:S(2)}) async-start(), calls=%async_computation.4 | async-start | bytes 2621440 | tf_op jit(solution)/shard_map/all_gather | solution.py:115
  8.7 74.6 %all-gather.18.cloned.1.call-start = ((), (), s32[]{:S(2)}) async-start(), calls=%async_computation.7 | async-start | bytes 2621440 | tf_op jit(solution)/shard_map/all_gather | solution.py:116
  9.4 149.9 %all-gather.14.cloned.1.call-start = ((), (), s32[]{:S(2)}) async-start(), calls=%async_computation.5 | async-start | bytes 4718592 | tf_op jit(solution)/shard_map/all_gather | solution.py:131
  15.0 51.4 %copy-start.25 = (f32[256,128]{0,1:T(8,128)}, f32[256,128]{0,1:T(8,128)S(1)}, u32[]{:S(2)}) copy-start(f32[256,128]{0,1:T(8,128)S(1)} %get-tuple-element.1101) | copy-start | bytes 393220
  16.3 67.0 %copy-start.36 = (f32[256]{0:T(256)}, f32[256]{0:T(256)S(1)}, u32[]{:S(2)}) copy-start(f32[256]{0:T(256)S(1)} %add_rsqrt_fusion.3) | copy-start | bytes 3076
  34.9 28.1 %copy-start.4 = (bf16[1,256,1024]{2,1,0:T(8,128)(2,1)S(1)}, bf16[1,256,1024]{2,1,0:T(8,128)(2,1)}, u32[]{:S(2)}) copy-start(bf16[1,256,1024]{2,1,0:T(8,128)(2,1)} %param.33) | copy-start | bytes 1572868
  34.9 28.1 %copy-start.34 = (f32[1024]{0:T(1024)S(1)}, f32[1024]{0:T(1024)}, u32[]{:S(2)}) copy-start(f32[1024]{0:T(1024)} %param.39) | copy-start | bytes 12292
  67.9 22.3 %copy-start.42 = (s32[4,2]{0,1:T(2,128)S(1)}, s32[4,2]{0,1:T(2,128)}, u32[]{:S(2)}) copy-start(s32[4,2]{0,1:T(2,128)} %param.47) | copy-start | bytes 100
  67.9 22.3 %copy-start.43 = (s32[4,2]{0,1:T(2,128)S(1)}, s32[4,2]{0,1:T(2,128)}, u32[]{:S(2)}) copy-start(s32[4,2]{0,1:T(2,128)} %param.49) | copy-start | bytes 100
  67.9 165.6 %all-gather.20.cloned.1.call-start = ((), (), s32[]{:S(2)}) async-start(), calls=%async_computation.8 | async-start | bytes 4718592 | tf_op jit(solution)/shard_map/all_gather | solution.py:132
  86.4 176.7 %all-gather.22.cloned.1.call-start = ((), (), s32[]{:S(2)}) async-start(), calls=%async_computation.9 | async-start | bytes 2621440 | tf_op jit(solution)/shard_map/all_gather | solution.py:117
  87.0 213.8 %all-gather.24.cloned.1.call-start = ((), (), s32[]{:S(2)}) async-start(), calls=%async_computation.10 | async-start | bytes 7208960 | tf_op jit(solution)/shard_map/all_gather | solution.py:203
  87.8 258.0 %all-gather.26.cloned.1.call-start = ((), (), s32[]{:S(2)}) async-start(), calls=%async_computation.11 | async-start | bytes 7208960 | tf_op jit(solution)/shard_map/all_gather | solution.py:204
  88.5 302.3 %all-gather.28.cloned.1.call-start = ((), (), s32[]{:S(2)}) async-start(), calls=%async_computation.12 | async-start | bytes 7208960 | tf_op jit(solution)/shard_map/all_gather | solution.py:205
  89.3 497.7 %reduce-scatter.5.cloned.1.call-start = ((), (), s32[]{:S(2)}) async-start(), calls=%async_computation.13 | async-start | bytes 4718592 | tf_op jit(solution)/shard_map/reduce_scatter | solution.py:286
  390.8 7.3 slice-start.4
  390.8 7.3 slice-start.5
  396.8 7.4 slice-start
  396.8 9.1 slice-start.2
  398.1 6.1 copy-start.23
  398.1 6.1 slice-start.1
  398.1 7.8 slice-start.3
  471.7 207.0 %reduce-scatter.7.cloned.1.call-start = ((), (), s32[]{:S(2)}) async-start(), calls=%async_computation.14 | async-start | bytes 4718592 | tf_op jit(solution)/shard_map/reduce_scatter | solution.py:289
  479.7 256.1 %reduce-scatter.11.cloned.1.call-start = ((), (), s32[]{:S(2)}) async-start(), calls=%async_computation.16 | async-start | bytes 7208960 | tf_op jit(solution)/shard_map/reduce_scatter | solution.py:325
  485.3 399.5 %reduce-scatter.9.cloned.1.call-start = ((), (), s32[]{:S(2)}) async-start(), calls=%async_computation.15 | async-start | bytes 24903680 | tf_op jit(solution)/shard_map/reduce_scatter | solution.py:319
  495.2 93.1 %copy-start.27 = (f32[256,128]{0,1:T(8,128)S(1)}, f32[256,128]{0,1:T(8,128)}, u32[]{:S(2)}) copy-start(f32[256,128]{0,1:T(8,128)} %get-tuple-element.1102) | copy-start | bytes 393220
  495.2 93.1 %copy-start.28 = (f32[256,128]{0,1:T(8,128)S(1)}, f32[256,128]{0,1:T(8,128)}, u32[]{:S(2)}) copy-start(f32[256,128]{0,1:T(8,128)} %get-tuple-element.1100) | copy-start | bytes 393220
  702.0 182.9 %copy-start.7 = (bf16[1024,1024]{1,0:T(8,128)(2,1)S(1)}, bf16[1024,1024]{1,0:T(8,128)(2,1)}, u32[]{:S(2)}) copy-start(bf16[1024,1024]{1,0:T(8,128)(2,1)} %all-gather.16.cloned.1.call-done) | copy-start | bytes 6291460
  702.0 273.2 %all-reduce.2.cloned.1.call-start = ((), (), s32[]{:S(2)}) async-start(), calls=%async_computation.17 | async-start | bytes 2883584 | tf_op jit(solution)/shard_map/psum | solution.py:333
  735.8 996.0 %all-gather.30.cloned.1.call-start = ((), (), s32[]{:S(2)}) async-start(), calls=%async_computation.18 | async-start | bytes 44826624 | tf_op jit(solution)/shard_map/all_gather | solution.py:332
  886.5 44.6 %copy-start.6 = (f32[256,1024]{1,0:T(8,128)S(1)}, f32[256,1024]{1,0:T(8,128)}, u32[]{:S(2)}) copy-start(f32[256,1024]{1,0:T(8,128)} %copy-done.5) | copy-start | bytes 3145732
  (49 other events, 134.6 us)
Sparse Core Ops, SparseCore 0:
  9.6 25.2 all-gather.15
  36.5 22.5 all-gather.11
  60.6 22.5 all-gather.17
  85.8 73.3 all-gather.13
  161.8 71.6 all-gather.19
  234.9 20.8 all-gather.21
  257.4 43.3 all-gather.23
  302.4 43.3 all-gather.25
  347.4 43.3 all-gather.27
  471.8 115.1 reduce-scatter.4
  591.0 87.6 reduce-scatter.6
  681.1 54.6 reduce-scatter.10
  738.5 146.2 reduce-scatter.8
  888.4 86.8 all-reduce.1
  976.7 754.9 all-gather.29
